TPU v7x, 32 devices: a whole 2x2x4 slice. The times are simulated.
32 devices in a mesh: expert: 4 (over z), tensor: 8 (over y, x, core).
Axes of the slice: x: 2, y: 2, z: 4, core: 2. Of those that a mesh axis runs over, the one named last changes fastest.
Arguments:
- tokens: bfloat16 [1024, 4096], P(('expert', 'tensor')), may hold values from -6 to 6
- router: float32 [4096, 4], replicated, may hold values from -0.09375 to 0.09375
- choice_ids: int32 [1024, 2], P(('expert', 'tensor')), may hold values from 0 to 3, all different within a row; in each aligned block of 32 rows (0 to 31, 32 to 63, ...) at most 20 rows name the same one
- w_gate: bfloat16 [4, 4096, 14336], P('expert', None, 'tensor'), may hold values from -0.09375 to 0.09375
- w_up: bfloat16 [4, 4096, 14336], P('expert', None, 'tensor'), may hold values from -0.09375 to 0.09375
- w_down: bfloat16 [4, 14336, 4096], P('expert', 'tensor'), may hold values from -0.046875 to 0.046875
Outputs:
- mixed: bfloat16 [1024, 4096], P(('expert', 'tensor'))
Inputs may be any that keep to these rules, and one draw needn't show every extreme that they name: `choice_ids`: the 2 experts of a token differ. In each aligned block of 32 rows (the rows of one device) each expert is named by at most 20 rows, a bound that some block reaches.
All inputs are finite; a program needn't handle non-finite values.
Results may differ from a plain program's by a relative error of at most 0.015.
Values may be sent and summed in bfloat16 or wider, within the bound.
No kernel may reach another device: no remote copies, remote signals or barrier semaphores. Data moves between devices by JAX's collectives and lax.ppermute only.
A program may use at most 128 MiB of HBM per device.

v0:
```python
import jax
import jax.numpy as jnp
from jax import lax
from jax.sharding import PartitionSpec as P


def hidden_units(row_piece, weight_gate, weight_up):
    gate_proj = jnp.dot(row_piece, weight_gate, preferred_element_type=jnp.float32)
    up_proj = jnp.dot(row_piece, weight_up, preferred_element_type=jnp.float32)
    return (jax.nn.silu(gate_proj) * up_proj).astype(jnp.bfloat16)


def on_device(tokens, router, choice_ids, w_gate, w_up, w_down):
    tok_count, feat_width = tokens.shape
    top_count = choice_ids.shape[1]
    experts = lax.axis_size("expert")
    capacity = tok_count * top_count * 5 // (experts * 4)
    group_rows = experts * capacity
    weight_gate = w_gate[0]
    weight_up = w_up[0]
    weight_down = w_down[0]
    logits = jnp.dot(tokens.astype(jnp.float32), router, precision=lax.Precision.HIGHEST)
    picked = jnp.take_along_axis(logits, choice_ids, axis=1)
    gate_weights = jax.nn.softmax(picked, axis=1)
    flat_ids = choice_ids.reshape(-1)
    onehot = (flat_ids[:, None] == jnp.arange(experts, dtype=jnp.int32)[None, :]).astype(jnp.int32)
    slot_rank = jnp.cumsum(onehot, axis=0) - onehot
    slot_index = jnp.sum(slot_rank * onehot, axis=1)
    destination = flat_ids * capacity + slot_index
    dispatch_map = (
        jnp.arange(group_rows, dtype=jnp.int32)[:, None] == destination[None, :]
    ).astype(jnp.bfloat16)
    doubled = jnp.repeat(tokens, top_count, axis=0)
    buffer = jnp.dot(dispatch_map, doubled, preferred_element_type=jnp.float32).astype(jnp.bfloat16)
    arrived = lax.all_to_all(buffer, "expert", split_axis=0, concat_axis=0, tiled=True)
    hidden = hidden_units(
        lax.all_gather(arrived, "tensor", axis=0, tiled=True), weight_gate, weight_up
    )
    partial_value = jnp.dot(hidden, weight_down, preferred_element_type=jnp.float32)
    summed = lax.psum(partial_value.astype(jnp.bfloat16), "tensor").astype(jnp.float32)
    own_rows = lax.dynamic_slice_in_dim(
        summed, lax.axis_index("tensor") * group_rows, group_rows, 0
    )
    expert_out = own_rows.astype(jnp.bfloat16)
    returned = lax.all_to_all(expert_out, "expert", split_axis=0, concat_axis=0, tiled=True)
    gathered = jnp.dot(dispatch_map.T, returned, preferred_element_type=jnp.float32).reshape(
        tok_count, top_count, feat_width
    )
    result = jnp.sum(gathered * gate_weights[:, :, None], axis=1)
    return result.astype(jnp.bfloat16)


def solution(mesh):
    in_specs = (
        P(("expert", "tensor"), None),
        P(),
        P(("expert", "tensor"), None),
        P("expert", None, "tensor"),
        P("expert", None, "tensor"),
        P("expert", "tensor", None),
    )
    out_specs = P(("expert", "tensor"), None)
    return jax.shard_map(
        on_device, mesh=mesh, in_specs=in_specs, out_specs=out_specs, check_vma=False
    )
```

profile of v0, /device:TPU:0, one launch (start us, length us, event | category | flops | bytes accessed | tf_op | source)
XLA Modules:
  0.0 253.6 jit_solution(12875386895920183099)
XLA Ops:
  6.5 0.8 copy.26
  7.3 0.1 reshape.74
  7.5 0.1 reduce_window_sum.11
  7.6 0.2 select_reduce_fusion
  7.8 1.4 broadcast_in_dim.6
  9.2 0.2 reshape.75
  9.5 0.3 convolution_convert_fusion
  9.8 0.1 all_to_all.16
  9.9 26.3 %all_to_all.24 = bf16[4,20,4096]{2,1,0:T(8,128)(2,1)S(1)} all-to-all(bf16[4,20,4096]{2,1,0:T(8,128)(2,1)S(1)} %all_to_all.16), channel_id=1, replica_groups=mesh['expert'=4,'tensor'=8] {'expert'}, dimensions={0} | all-to-all | bytes 1310720 | tf_op jit(solution)/shard_map/all_to_all | solution.py:35
  36.2 1.0 all_to_all.18
  37.3 40.2 %all-gather.2.cloned.1.call-done = bf16[640,4096]{1,0:T(8,128)(2,1)} async-done(((bf16[80,4096]{1,0:T(8,128)(2,1)}), bf16[640,4096]{1,0:T(8,128)(2,1)}) %all-gather.2.cloned.1.call-update) | async-done | bytes 5242896 | tf_op jit(solution)/shard_map/all_gather | solution.py:37
  77.4 15.9 %fusion.4 = f32[640,1792]{1,0:T(8,128)} fusion(bf16[640,4096]{1,0:T(8,128)(2,1)} %all-gather.2.cloned.1.call-done, bf16[1,4096,1792]{2,1,0:T(8,128)(2,1)} %param.9), kind=kOutput, calls=%fused_computation.5 | convolution fusion | flops 9395240960 | bytes 24510464 | tf_op jit(solution)/shard_map/dot_general | solution.py:8
  93.3 33.1 %fusion.6 = bf16[640,4096]{1,0:T(8,128)(2,1)} fusion(bf16[1,1792,4096]{2,1,0:T(8,128)(2,1)} %param.11, f32[640,1792]{1,0:T(8,128)} %fusion.4, bf16[640,4096]{1,0:T(8,128)(2,1)} %all-gather.2.cloned.1.call-done, bf16[1,4096,1792]{2,1,0:T(8,128)(2,1)} %param.10), kind=kOutput, calls=%fused_computation.7 | convolution fusion | flops 18799984640 | bytes 44433408 | tf_op jit(solution)/shard_map/dot_general | solution.py:39
  126.5 0.6 copy-done.2
  127.2 0.1 reshape.77
  127.4 91.7 %all-reduce.2.cloned.1.call-done = bf16[640,4096]{1,0:T(8,128)(2,1)} async-done(((bf16[640,4096]{1,0:T(8,128)(2,1)}), bf16[640,4096]{1,0:T(8,128)(2,1)}) %all-reduce.2.cloned.1.call-update) | async-done | bytes 5242896 | tf_op jit(solution)/shard_map/psum | solution.py:40
  219.0 1.1 convert_convert_fusion
  220.1 1.0 all_to_all.19
  221.2 4.6 %all-to-all-start.1 = ((bf16[4,20,4096]{2,1,0:T(8,128)(2,1)}), bf16[4,20,4096]{2,1,0:T(8,128)(2,1)S(1)}, u32[]{:S(2)}, u32[]{:S(2)}) async-start(bf16[4,20,4096]{2,1,0:T(8,128)(2,1)} %all_to_all.19), calls=%async_computation.1 | async-start | bytes 1572864 | tf_op jit(solution)/shard_map/all_to_all | solution.py:45
  225.8 0.3 fusion.22
  226.1 0.9 gather_fusion
  227.3 18.3 %all-to-all-done.1 = bf16[4,20,4096]{2,1,0:T(8,128)(2,1)S(1)} async-done(((bf16[4,20,4096]{2,1,0:T(8,128)(2,1)}), bf16[4,20,4096]{2,1,0:T(8,128)(2,1)S(1)}, u32[]{:S(2)}, u32[]{:S(2)}) %all-to-all-start.1) | async-done | bytes 655392 | tf_op jit(solution)/shard_map/all_to_all | solution.py:45
  245.6 0.1 reshape.88
  245.8 1.0 fusion.14
  (24 shorter events, 0.6 us)
Async XLA Ops:
  6.5 219.2 %copy-start = (f32[4096,4]{0,1:T(4,128)S(1)}, f32[4096,4]{0,1:T(4,128)}, u32[]{:S(2)}) copy-start(f32[4096,4]{0,1:T(4,128)} %param.7) | copy-start | bytes 196612
  6.5 70.9 %all-gather.2.cloned.1.call-start = ((), (), s32[]{:S(2)}) async-start(), calls=%async_computation.2 | async-start | bytes 5898240 | tf_op jit(solution)/shard_map/all_gather | solution.py:37
  7.8 2.0 copy-start.3
  37.2 181.8 %all-reduce.2.cloned.1.call-start = ((), (), s32[]{:S(2)}) async-start(), calls=%async_computation.3 | async-start | bytes 10485760 | tf_op jit(solution)/shard_map/psum | solution.py:40
  126.5 0.7 copy-start.2
  126.5 99.3 %copy-start.1 = (bf16[32,4096]{1,0:T(8,128)(2,1)S(1)}, bf16[32,4096]{1,0:T(8,128)(2,1)}, u32[]{:S(2)}) copy-start(bf16[32,4096]{1,0:T(8,128)(2,1)} %param.6) | copy-start | bytes 786436
  221.2 24.4 %all-to-all-start.1 = ((bf16[4,20,4096]{2,1,0:T(8,128)(2,1)}), bf16[4,20,4096]{2,1,0:T(8,128)(2,1)S(1)}, u32[]{:S(2)}, u32[]{:S(2)}) async-start(bf16[4,20,4096]{2,1,0:T(8,128)(2,1)} %all_to_all.19), calls=%async_computation.1 | async-start | bytes 1572864 | tf_op jit(solution)/shard_map/all_to_all | solution.py:45
  226.1 1.1 copy-start.4
Sparse Core Ops, SparseCore 0:
  37.3 40.0 all-gather.1
  126.6 92.3 all-reduce.1
where the time goes:
time: 254 us
  waiting for transfers between devices  150 us (59%)
  matrix products  50.6 us (20%)
  blocking collectives  26.3 us (10%)
  between operations  13.5 us (5%)
  local copies, waits for them, and re-layouts  6.75 us (3%)
  starting transfers between devices  4.64 us (2%)
    psum x1, waiting for transfers between devices, on_device(): lax.psum(partial_value.astype(jnp.bfloat16), 'tensor').astype(jnp.float32)  91.7 us
    all_gather x1, waiting for transfers between devices, on_device(): lax.all_gather(arrived, 'tensor', axis=0, tiled=True)  40.2 us
    dot_general x1, matrix products, on_device(): jnp.dot(hidden, weight_down, preferred_element_type=jnp.float32)  33.1 us
    all_to_all x1, blocking collectives, on_device(): lax.all_to_all(buffer, 'expert', split_axis=0, concat_axis=0, tiled=True)  26.3 us
    all_to_all x1, waiting for transfers between devices, on_device(): lax.all_to_all(expert_out, 'expert', split_axis=0, concat_axis=0, tiled=T...  18.3 us
    dot_general x1, matrix products, hidden_units(): jnp.dot(row_piece, weight_gate, preferred_element_type=jnp.float32)  15.9 us
  transfers between devices with their start and end apart: 3, of which 3 were waited for; matrix products, arithmetic and copies ran while one was open for 1% of the time, Pallas kernels for 0%

commit v1 on v0

--- a/solution.py
+++ b/solution.py
@@ -2,6 +2,12 @@
 import jax.numpy as jnp
 from jax import lax
 from jax.sharding import PartitionSpec as P
+
+
+def add_all(x, name):
+    shards = lax.all_gather(x, name, axis=0, tiled=False)
+    total = shards.sum(axis=0)
+    return total
 
 
 def hidden_units(row_piece, weight_gate, weight_up):
@@ -37,7 +43,7 @@
         lax.all_gather(arrived, "tensor", axis=0, tiled=True), weight_gate, weight_up
     )
     partial_value = jnp.dot(hidden, weight_down, preferred_element_type=jnp.float32)
-    summed = lax.psum(partial_value.astype(jnp.bfloat16), "tensor").astype(jnp.float32)
+    summed = add_all(partial_value.astype(jnp.bfloat16), "tensor").astype(jnp.float32)
     own_rows = lax.dynamic_slice_in_dim(
         summed, lax.axis_index("tensor") * group_rows, group_rows, 0
     )

time: 254 us -> 376 us (1.48)
  waiting for transfers between devices: 150 us -> 255 us
  other arithmetic: 1.63 us -> 18.7 us
    all_gather x0 -> x1, waiting for transfers between devices: none -> 196 us  [add_all(): shards = lax.all_gather(x, name, axis=0, tiled=False)]
    psum x1 -> x0, waiting for transfers between devices: 91.7 us -> none  [on_device(): lax.psum(partial_value.astype(jnp.bfloat16), 'tensor').astype(jnp.float32)]
    reduce_sum x0 -> x1, other arithmetic: none -> 17.1 us  [add_all(): total = shards.sum(axis=0)]
  transfers between devices with their start and end apart: 3 -> 3, of which waited for: 3 -> 3; matrix products, arithmetic and copies ran while one was open for 1% -> 0% of each run, Pallas kernels for 0% -> 0%
where the time goes in v1:
time: 376 us
  waiting for transfers between devices  255 us (68%)
  matrix products  50.6 us (13%)
  blocking collectives  26.3 us (7%)
  other arithmetic  18.7 us (5%)
  between operations  13.5 us (4%)
  local copies, waits for them, and re-layouts  6.76 us (2%)
  starting transfers between devices  4.64 us (1%)
    all_gather x1, waiting for transfers between devices, add_all(): shards = lax.all_gather(x, name, axis=0, tiled=False)  196 us
    all_gather x1, waiting for transfers between devices, on_device(): lax.all_gather(arrived, 'tensor', axis=0, tiled=True)  40.2 us
    dot_general x1, matrix products, on_device(): jnp.dot(hidden, weight_down, preferred_element_type=jnp.float32)  33.1 us
    all_to_all x1, blocking collectives, on_device(): lax.all_to_all(buffer, 'expert', split_axis=0, concat_axis=0, tiled=True)  26.3 us
    all_to_all x1, waiting for transfers between devices, on_device(): lax.all_to_all(expert_out, 'expert', split_axis=0, concat_axis=0, tiled=T...  18.9 us
    reduce_sum x1, other arithmetic, add_all(): total = shards.sum(axis=0)  17.1 us
    dot_general x1, matrix products, hidden_units(): jnp.dot(row_piece, weight_gate, preferred_element_type=jnp.float32)  15.8 us
  transfers between devices with their start and end apart: 3, of which 3 were waited for; matrix products, arithmetic and copies ran while one was open for 0% of the time, Pallas kernels for 0%

profile of v1, /device:TPU:0, one launch (start us, length us, event | category | flops | bytes accessed | tf_op | source)
XLA Modules:
  0.0 376.0 jit_solution(168362081173735605)
XLA Ops:
  6.5 0.8 copy.26
  7.3 0.1 reshape.74
  7.6 0.2 select_reduce_fusion
  7.8 1.4 broadcast_in_dim.6
  9.2 0.2 reshape.75
  9.5 0.3 convolution_convert_fusion
  9.8 0.1 all_to_all.16
  9.9 26.3 %all_to_all.24 = bf16[4,20,4096]{2,1,0:T(8,128)(2,1)S(1)} all-to-all(bf16[4,20,4096]{2,1,0:T(8,128)(2,1)S(1)} %all_to_all.16), channel_id=1, replica_groups=mesh['expert'=4,'tensor'=8] {'expert'}, dimensions={0} | all-to-all | bytes 1310720 | tf_op jit(solution)/shard_map/all_to_all | solution.py:41
  36.2 1.0 all_to_all.18
  37.3 40.2 %all-gather.4.cloned.1.call-done = bf16[640,4096]{1,0:T(8,128)(2,1)} async-done(((bf16[80,4096]{1,0:T(8,128)(2,1)}), bf16[640,4096]{1,0:T(8,128)(2,1)}) %all-gather.4.cloned.1.call-update) | async-done | bytes 5242896 | tf_op jit(solution)/shard_map/all_gather | solution.py:43
  77.5 15.8 %fusion.4 = f32[640,1792]{1,0:T(8,128)} fusion(bf16[640,4096]{1,0:T(8,128)(2,1)} %all-gather.4.cloned.1.call-done, bf16[1,4096,1792]{2,1,0:T(8,128)(2,1)} %param.9), kind=kOutput, calls=%fused_computation.5 | convolution fusion | flops 9395240960 | bytes 24510464 | tf_op jit(solution)/shard_map/dot_general | solution.py:14
  93.3 33.1 %fusion.6 = bf16[640,4096]{1,0:T(8,128)(2,1)} fusion(bf16[1,1792,4096]{2,1,0:T(8,128)(2,1)} %param.11, f32[640,1792]{1,0:T(8,128)} %fusion.4, bf16[640,4096]{1,0:T(8,128)(2,1)} %all-gather.4.cloned.1.call-done, bf16[1,4096,1792]{2,1,0:T(8,128)(2,1)} %param.10), kind=kOutput, calls=%fused_computation.7 | convolution fusion | flops 18799984640 | bytes 44433408 | tf_op jit(solution)/shard_map/dot_general | solution.py:45
  126.4 0.6 copy-done.2
  127.2 0.1 reshape.77
  127.3 196.3 %all-gather.6.cloned.1.call-done = bf16[5120,4096]{1,0:T(8,128)(2,1)} async-done(((bf16[640,4096]{1,0:T(8,128)(2,1)}), bf16[5120,4096]{1,0:T(8,128)(2,1)}) %all-gather.6.cloned.1.call-update) | async-done | bytes 41943056 | tf_op jit(solution)/shard_map/all_gather | solution.py:8
  323.6 17.1 %reduce_sum.40 = bf16[640,4096]{1,0:T(8,128)(2,1)} reduce(bf16[8,640,4096]{2,1,0:T(8,128)(2,1)} %bitcast.26, bf16[]{:T(256)} %constant.21.clone.1), dimensions={0}, to_apply=%region_2.3 | reduce | flops 18350080 | bytes 47185920 | tf_op jit(solution)/shard_map/reduce_sum | solution.py:9
  340.7 1.1 convert_convert_fusion
  341.8 1.0 all_to_all.19
  342.9 4.6 %all-to-all-start.1 = ((bf16[4,20,4096]{2,1,0:T(8,128)(2,1)}), bf16[4,20,4096]{2,1,0:T(8,128)(2,1)S(1)}, u32[]{:S(2)}, u32[]{:S(2)}) async-start(bf16[4,20,4096]{2,1,0:T(8,128)(2,1)} %all_to_all.19), calls=%async_computation.1 | async-start | bytes 1572864 | tf_op jit(solution)/shard_map/all_to_all | solution.py:51
  347.5 0.3 fusion.22
  347.8 0.9 gather_fusion
  349.0 18.9 %all-to-all-done.1 = bf16[4,20,4096]{2,1,0:T(8,128)(2,1)S(1)} async-done(((bf16[4,20,4096]{2,1,0:T(8,128)(2,1)}), bf16[4,20,4096]{2,1,0:T(8,128)(2,1)S(1)}, u32[]{:S(2)}, u32[]{:S(2)}) %all-to-all-start.1) | async-done | bytes 655392 | tf_op jit(solution)/shard_map/all_to_all | solution.py:51
  368.0 0.1 reshape.89
  368.1 1.0 fusion.14
  (25 shorter events, 0.7 us)
Async XLA Ops:
  6.5 340.9 %copy-start = (f32[4096,4]{0,1:T(4,128)S(1)}, f32[4096,4]{0,1:T(4,128)}, u32[]{:S(2)}) copy-start(f32[4096,4]{0,1:T(4,128)} %param.7) | copy-start | bytes 196612
  6.5 70.9 %all-gather.4.cloned.1.call-start = ((), (), s32[]{:S(2)}) async-start(), calls=%async_computation.2 | async-start | bytes 5898240 | tf_op jit(solution)/shard_map/all_gather | solution.py:43
  7.8 2.0 copy-start.3
  37.2 286.4 %all-gather.6.cloned.1.call-start = ((), (), s32[]{:S(2)}) async-start(), calls=%async_computation.3 | async-start | bytes 47185920 | tf_op jit(solution)/shard_map/all_gather | solution.py:8
  126.4 0.7 copy-start.2
  323.6 23.9 %copy-start.1 = (bf16[32,4096]{1,0:T(8,128)(2,1)S(1)}, bf16[32,4096]{1,0:T(8,128)(2,1)}, u32[]{:S(2)}) copy-start(bf16[32,4096]{1,0:T(8,128)(2,1)} %param.6) | copy-start | bytes 786436
  342.9 25.1 %all-to-all-start.1 = ((bf16[4,20,4096]{2,1,0:T(8,128)(2,1)}), bf16[4,20,4096]{2,1,0:T(8,128)(2,1)S(1)}, u32[]{:S(2)}, u32[]{:S(2)}) async-start(bf16[4,20,4096]{2,1,0:T(8,128)(2,1)} %all_to_all.19), calls=%async_computation.1 | async-start | bytes 1572864 | tf_op jit(solution)/shard_map/all_to_all | solution.py:51
  347.8 1.1 copy-start.4
Sparse Core Ops, SparseCore 0:
  37.3 40.0 all-gather.3
  126.6 196.9 all-gather.5
